TPU v7x, 32 devices: a whole 2x2x4 slice. The times are simulated.
32 devices in a mesh: leaf: 8 (over z, y), rows: 4 (over x, core).
Axes of the slice: x: 2, y: 2, z: 4, core: 2. Of those that a mesh axis runs over, the one named last changes fastest.
Arguments:
- sigma_top: float32 [2048, 1024], P('leaf'), may hold values from -4 to 40, as said below
- panel_top: float32 [1024, 12288], P(None, 'leaf'), may hold values from -0.125 to 0.125
- diag_top: float32 [12288, 256], P('leaf'), may hold values from -4 to 20, as said below
- panel_mid: float32 [1024, 24576], P(None, ('leaf', 'rows')), may hold values from -0.125 to 0.125
- diag_mid: float32 [24576, 256], P(('leaf', 'rows')), may hold values from -4 to 20, as said below
- pattern_mid: int32 [4, 4], replicated, may hold values from 0 to 23, as said below
- panel_low: float32 [1024, 49152], P(None, ('leaf', 'rows')), may hold values from -0.125 to 0.125
- diag_low: float32 [49152, 256], P(('leaf', 'rows')), may hold values from -4 to 20, as said below
- pattern_low: int32 [8, 4], replicated, may hold values from 0 to 23, as said below
Outputs:
- cross_top: float32 [1024, 12288], P('rows', 'leaf')
- marginal_top: float32 [12288, 256], P(('leaf', 'rows'))
- cross_mid: float32 [1024, 24576], P(None, ('leaf', 'rows'))
- marginal_mid: float32 [24576, 256], P(('leaf', 'rows'))
- cross_low: float32 [1024, 49152], P(None, ('leaf', 'rows'))
- marginal_low: float32 [49152, 256], P(('leaf', 'rows'))
Inputs may be any that keep to these rules, and one draw needn't show every extreme that they name: Each block of 1024 rows of sigma_top is symmetric. `diag_top`: each 256 x 256 block is symmetric. `diag_mid`: each block of 256 rows is symmetric. `diag_low`: each block of 256 rows is symmetric. `pattern_mid`: the 4 entries of a row are different; rows 2i and 2i + 1 together name 8 different blocks. `pattern_low`: the 4 entries of a row are different; rows 2i and 2i + 1 together name 8 different blocks.
All inputs are finite; a program needn't handle non-finite values.
Results may differ from a plain program's by a relative error of at most 0.00009.
Values sent between devices are 32-bit elements; how exact they have to be, the bound alone decides.
A program may use at most 192 MiB of HBM per device.

v0:
```python
import jax
import jax.numpy as jnp
from jax import lax
from jax.sharding import PartitionSpec as P

HIGH = lax.Precision.HIGHEST


def from_partner(value, axis, bit):
    return lax.ppermute(value, axis, [(i, i ^ 1 << bit) for i in range(lax.axis_size(axis))])


def block_diagonal(blocks):
    block_count = blocks.shape[0]
    block_side = blocks.shape[1]
    eye_table = jnp.eye(block_count, dtype=blocks.dtype)
    spread_out = blocks[:, :, None, :] * eye_table[:, None, :, None]
    return spread_out.reshape(block_count * block_side, block_count * block_side)


def select_blocks(panel_cols, diag_blocks, wanted, owned_mask, block_size):
    rows_total = panel_cols.shape[0]
    local_count = panel_cols.shape[1] // block_size
    taken_blocks = (
        jnp.take(panel_cols.reshape(rows_total, local_count, block_size), wanted, axis=1)
        * owned_mask[None, :, None]
    )
    taken_diag = (
        jnp.take(diag_blocks.reshape(local_count, block_size, block_size), wanted, axis=0)
        * owned_mask[:, None, None]
    )
    return (taken_blocks.reshape(rows_total, -1), taken_diag.reshape(-1, block_size))


def child_cov(parent_cov, chosen, chosen_diag, block_size):
    block_count = chosen_diag.shape[0] // block_size
    product = jnp.dot(parent_cov, chosen, precision=HIGH, preferred_element_type=jnp.float32)
    inner_part = jnp.dot(chosen.T, product, precision=HIGH, preferred_element_type=jnp.float32)
    return inner_part + block_diagonal(chosen_diag.reshape(block_count, block_size, block_size))


def marg_terms(panel_cols, cover_cols, block_size):
    rows_total = panel_cols.shape[0]
    block_count = panel_cols.shape[1] // block_size
    terms = jnp.einsum(
        "sai,saj->aij",
        panel_cols.reshape(rows_total, block_count, block_size),
        cover_cols.reshape(rows_total, block_count, block_size),
        precision=HIGH,
    )
    return terms.reshape(block_count * block_size, block_size)


def quad_total(pieces):
    for bit_number in range(2):
        others = from_partner((pieces[0], pieces[1], pieces[2]), "leaf", bit_number)
        pieces = (pieces[0] + others[0], pieces[1] + others[1], pieces[2] + others[2])
    return pieces


def local(
    sigma_top,
    panel_top,
    diag_top,
    panel_mid,
    diag_mid,
    pattern_mid,
    panel_low,
    diag_low,
    pattern_low,
):
    block_size = diag_top.shape[1]
    struct_rows = panel_top.shape[0]
    row_count = lax.axis_size("rows")
    leaf_index = lax.axis_index("leaf")
    rows_index = lax.axis_index("rows")
    slot_blocks = pattern_mid.shape[1]
    slot_width = slot_blocks * block_size
    quad_place = leaf_index % 4
    quad_number = leaf_index // 4
    top_local = panel_top.shape[1] // block_size
    children = 2 * quad_number + jnp.arange(2, dtype=jnp.int32)
    wanted_top = pattern_mid[children].reshape(-1)
    owned_top = (wanted_top // top_local == quad_place).astype(jnp.float32)
    chosen_top, chosen_top_diag = select_blocks(
        panel_top, diag_top, wanted_top % top_local, owned_top, block_size
    )
    padded_cov = lax.dynamic_update_slice_in_dim(
        jnp.zeros((struct_rows, struct_rows), jnp.float32),
        sigma_top,
        quad_place * sigma_top.shape[0],
        0,
    )
    share_rows = struct_rows // row_count
    diag_share = chosen_top_diag.shape[0] // row_count
    pieces = (
        lax.dynamic_slice_in_dim(padded_cov, rows_index * share_rows, share_rows, 0),
        lax.dynamic_slice_in_dim(chosen_top, rows_index * share_rows, share_rows, 0),
        lax.dynamic_slice_in_dim(chosen_top_diag, rows_index * diag_share, diag_share, 0),
    )
    pieces = quad_total(pieces)
    parent_cov, chosen_all, chosen_diag_all = (
        lax.all_gather(pieces[0], "rows", axis=0, tiled=True),
        lax.all_gather(pieces[1], "rows", axis=0, tiled=True),
        lax.all_gather(pieces[2], "rows", axis=0, tiled=True),
    )
    mid_local = panel_mid.shape[1] // block_size
    pair_number = leaf_index // 2
    pair_place = leaf_index % 2 * row_count + rows_index
    low_children = 2 * pair_number + jnp.arange(2, dtype=jnp.int32)
    wanted_mid = pattern_low[low_children].reshape(-1)
    owned_mid = (wanted_mid // mid_local == pair_place).astype(jnp.float32)
    chosen_mid, chosen_mid_diag = select_blocks(
        panel_mid, diag_mid, wanted_mid % mid_local, owned_mid, block_size
    )
    summed = lax.psum((chosen_mid, chosen_mid_diag), "rows")
    partner = from_partner((summed[0], summed[1]), "leaf", 0)
    mid_all = summed[0] + partner[0]
    mid_diag_all = summed[1] + partner[1]
    share_struct = struct_rows // row_count
    cov_rows = lax.dynamic_slice_in_dim(parent_cov, rows_index * share_struct, share_struct, 0)
    cross_top = -jnp.dot(cov_rows, panel_top, precision=HIGH, preferred_element_type=jnp.float32)
    panel_rows = lax.dynamic_slice_in_dim(panel_top, rows_index * share_struct, share_struct, 0)
    partial_value = marg_terms(panel_rows, cross_top, block_size)
    piece_rows = partial_value.shape[0] // row_count
    own_diag = lax.dynamic_slice_in_dim(diag_top, rows_index * piece_rows, piece_rows, 0)
    summed_terms = lax.psum(partial_value, "rows")
    marginal_top = own_diag - lax.dynamic_slice_in_dim(
        summed_terms, rows_index * piece_rows, piece_rows, 0
    )
    child_place = leaf_index // 2 % 2
    own_slots = lax.dynamic_slice_in_dim(chosen_all, child_place * slot_width, slot_width, 1)
    own_slot_diag = lax.dynamic_slice_in_dim(
        chosen_diag_all, child_place * slot_width, slot_width, 0
    )
    mid_cov = child_cov(parent_cov, own_slots, own_slot_diag, block_size)
    cross_mid = -jnp.dot(mid_cov, panel_mid, precision=HIGH, preferred_element_type=jnp.float32)
    marginal_mid = diag_mid - marg_terms(panel_mid, cross_mid, block_size)
    low_place = leaf_index % 2
    low_slots = lax.dynamic_slice_in_dim(mid_all, low_place * slot_width, slot_width, 1)
    low_slot_diag = lax.dynamic_slice_in_dim(mid_diag_all, low_place * slot_width, slot_width, 0)
    low_cov = child_cov(mid_cov, low_slots, low_slot_diag, block_size)
    cross_low = -jnp.dot(low_cov, panel_low, precision=HIGH, preferred_element_type=jnp.float32)
    marginal_low = diag_low - marg_terms(panel_low, cross_low, block_size)
    return (cross_top, marginal_top, cross_mid, marginal_mid, cross_low, marginal_low)


def solution(mesh):
    return jax.shard_map(
        local,
        mesh=mesh,
        in_specs=(
            P("leaf", None),
            P(None, "leaf"),
            P("leaf", None),
            P(None, ("leaf", "rows")),
            P(("leaf", "rows"), None),
            P(),
            P(None, ("leaf", "rows")),
            P(("leaf", "rows"), None),
            P(),
        ),
        out_specs=(
            P("rows", "leaf"),
            P(("leaf", "rows"), None),
            P(None, ("leaf", "rows")),
            P(("leaf", "rows"), None),
            P(None, ("leaf", "rows")),
            P(("leaf", "rows"), None),
        ),
        check_vma=False,
    )
```

profile of v0, /device:TPU:0, one launch (start us, length us, event | category | flops | bytes accessed | tf_op | source)
XLA Modules:
  0.0 711.9 jit_solution(2259707078649836408)
XLA Ops:
  11.7 23.2 %collective-permute-done = f32[256,1024]{1,0:T(8,128)S(1)} collective-permute-done((f32[256,1024]{1,0:T(8,128)S(1)}, f32[256,1024]{1,0:T(8,128)S(1)}, u32[]{:S(2)}, u32[]{:S(2)}) %collective-permute-start) | collective-permute-done | bytes 1048608 | tf_op jit(solution)/shard_map/ppermute | solution.py:10
  36.9 22.5 %collective-permute-done.1 = f32[256,1024]{1,0:T(8,128)S(1)} collective-permute-done((f32[256,1024]{1,0:T(8,128)S(1)}, f32[256,1024]{1,0:T(8,128)S(1)}, u32[]{:S(2)}, u32[]{:S(2)}) %collective-permute-start.1) | collective-permute-done | bytes 1048608 | tf_op jit(solution)/shard_map/ppermute | solution.py:10
  71.3 9.2 %copy.46 = f32[1024,8,256]{0,2,1:T(8,128)} copy(f32[1024,8,256]{2,0,1:T(8,128)} %bitcast.66) | data formatting | bytes 16777216 | tf_op jit(solution)/shard_map/jit(_take)/gather | solution.py:25
  86.5 5.9 fusion
  96.4 7.9 %convolution_negate_fusion.1 = f32[256,1536]{1,0:T(8,128)S(1)} fusion(f32[1024,1536]{1,0:T(8,128)} %param.10, f32[1024,1024]{1,0:T(8,128)} %all-gather.4.cloned.1.call-done, s32[]{:T(128)S(6)} %select_n.181), kind=kOutput, calls=%fused_computation.15 | convolution fusion | flops 4832231424 | bytes 8912900 | tf_op jit(solution)/shard_map/dot_general | solution.py:122
  110.5 6.6 copy.39
  117.8 6.6 copy.40
  124.4 7.1 %gather_fusion.1 = f32[8,1024,256]{2,1,0:T(8,128)} fusion(f32[1024,6,256]{2,0,1:T(8,128)} %copy.40, s32[1024]{0:T(1024)S(1)} %pad_clamp_fusion.2), kind=kCustom, calls=%fused_computation.1 | custom fusion | bytes 16777248 | tf_op jit(solution)/shard_map/jit(_take)/gather | solution.py:25
  131.5 9.2 %copy.41 = f32[1024,8,256]{0,2,1:T(8,128)} copy(f32[1024,8,256]{2,0,1:T(8,128)} %bitcast.67) | data formatting | bytes 16777216 | tf_op jit(solution)/shard_map/jit(_take)/gather | solution.py:25
  148.6 54.6 %collective-permute-done.4 = f32[512,256]{1,0:T(8,128)S(1)} collective-permute-done((f32[512,256]{1,0:T(8,128)S(1)}, f32[512,256]{1,0:T(8,128)S(1)}, u32[]{:S(2)}, u32[]{:S(2)}) %collective-permute-start.4) | collective-permute-done | bytes 524320 | tf_op jit(solution)/shard_map/ppermute | solution.py:10
  205.1 11.6 %collective-permute-done.5 = f32[512,256]{1,0:T(8,128)S(1)} collective-permute-done((f32[512,256]{1,0:T(8,128)S(1)}, f32[512,256]{1,0:T(8,128)S(1)}, u32[]{:S(2)}, u32[]{:S(2)}) %collective-permute-start.5) | collective-permute-done | bytes 524320 | tf_op jit(solution)/shard_map/ppermute | solution.py:10
  221.9 44.5 %collective-permute-done.3 = f32[256,2048]{0,1:T(8,128)S(1)} collective-permute-done((f32[256,2048]{0,1:T(8,128)S(1)}, f32[256,2048]{0,1:T(8,128)S(1)}, u32[]{:S(2)}, u32[]{:S(2)}) %collective-permute-start.3) | collective-permute-done | bytes 2097184 | tf_op jit(solution)/shard_map/ppermute | solution.py:10
  268.1 54.4 %all-reduce.3.cloned.1.call-done = (f32[1536,256]{1,0:T(8,128)}, f32[1024,2048]{0,1:T(8,128)}, f32[2048,256]{1,0:T(8,128)}) async-done(((f32[1536,256]{1,0:T(8,128)}, f32[1024,2048]{0,1:T(8,128)}, f32[2048,256]{1,0:T(8,128)}), (f32[1536,256]{1,0:T(8,128)}, f32[1024,2048]{0,1:T(8,128)}, f32[2048,256]{1,0:T(8,128)})) %all-reduce.3.cloned.1.call-update) | async-done | bytes 12058640 | tf_op jit(solution)/shard_map/psum | solution.py:127
  324.5 6.7 copy.48
  331.2 16.3 %all-gather.8.cloned.1.call-done = f32[2048,256]{1,0:T(8,128)} async-done(((f32[512,256]{1,0:T(8,128)}), f32[2048,256]{1,0:T(8,128)}) %all-gather.8.cloned.1.call-update) | async-done | bytes 2097168 | tf_op jit(solution)/shard_map/all_gather | solution.py:105
  350.7 198.7 %collective-permute-done.7 = f32[2048,256]{1,0:T(8,128)} collective-permute-done((f32[2048,256]{1,0:T(8,128)}, f32[2048,256]{1,0:T(8,128)}, u32[]{:S(2)}, u32[]{:S(2)}) %collective-permute-start.7) | collective-permute-done | bytes 2097184 | tf_op jit(solution)/shard_map/ppermute | solution.py:10
  558.5 25.9 %fusion.4 = f32[1024,1024]{1,0:T(8,128)S(1)} fusion(f32[1024,1024]{1,0:T(8,128)} %all-gather.4.cloned.1.call-done, f32[1024,2048]{0,1:T(8,128)} %all-gather.6.cloned.1.call-done, s32[]{:T(128)S(6)} %select_n.193), kind=kOutput, calls=%fused_computation.13 | convolution fusion | flops 12884901888 | bytes 12582916 | tf_op jit(solution)/shard_map/dot_general | solution.py:37
  584.4 14.0 %fusion.8 = f32[1024,1024]{1,0:T(8,128)S(1)} fusion(f32[1024,1024]{1,0:T(8,128)S(1)} %bitcast.75, f32[1024,1024]{1,0:T(8,128)S(1)} %fusion.4, f32[1024,2048]{0,1:T(8,128)S(1)} %copy-done.13, s32[]{:T(128)S(6)} %select_n.193), kind=kOutput, calls=%fused_computation.22 | convolution fusion | flops 12885950464 | bytes 16777220 | tf_op jit(solution)/shard_map/dot_general | solution.py:38
  600.4 12.4 %convolution_negate_fusion.2 = f32[1024,768]{0,1:T(8,128)} fusion(f32[1024,1024]{1,0:T(8,128)S(1)} %fusion.8, f32[1024,768]{1,0:T(8,128)S(1)} %copy-done.12), kind=kOutput, calls=%fused_computation.23 | convolution fusion | flops 9664462848 | bytes 10485760 | tf_op jit(solution)/shard_map/dot_general | solution.py:137
  623.3 17.4 %fusion.11 = f32[1024,1024]{1,0:T(8,128)S(1)} fusion(f32[1024,1024]{1,0:T(8,128)S(1)} %copy-done.4, f32[1024,2048]{0,1:T(8,128)} %collective-permute-done.6, s32[]{:T(128)S(6)} %select_n.204, f32[1024,2048]{0,1:T(8,128)} %get-tuple-element.25), kind=kOutput, calls=%fused_computation.25 | convolution fusion | flops 12885950464 | bytes 16777220 | tf_op jit(solution)/shard_map/dot_general | solution.py:37
  640.8 16.3 %fusion.12 = f32[1024,1024]{1,0:T(8,128)S(1)} fusion(f32[1024,1024]{1,0:T(8,128)S(1)} %fusion.11, f32[1024,2048]{0,1:T(8,128)} %collective-permute-done.6, s32[]{:T(128)S(6)} %select_n.204, f32[1024,2048]{0,1:T(8,128)S(1)} %bitcast.81), kind=kOutput, calls=%fused_computation.26 | convolution fusion | flops 12885950464 | bytes 16777220 | tf_op jit(solution)/shard_map/dot_general | solution.py:38
  657.1 22.3 %convolution_negate_fusion = f32[1024,1536]{1,0:T(8,128)} fusion(f32[1024,1536]{1,0:T(8,128)S(1)} %bitcast.83, f32[1024,1024]{1,0:T(8,128)S(1)} %fusion.12, f32[1024,1024]{1,0:T(8,128)S(1)} %bitcast.89), kind=kOutput, calls=%fused_computation.8 | convolution fusion | flops 19329974272 | bytes 20971520 | tf_op jit(solution)/shard_map/dot_general | solution.py:143
  679.4 6.6 copy.47
  686.0 17.6 %fusion.27 = f32[6,256,256]{1,2,0:T(8,128)S(1)} fusion(f32[1024,6,256]{0,2,1:T(8,128)} %bitcast.72, f32[1024,6,256]{0,2,1:T(8,128)} %bitcast.70), kind=kOutput, calls=%fused_computation.78 | convolution fusion | flops 4831838208 | bytes 14155776 | tf_op jit(solution)/shard_map/sai,saj->aij/dot_general | solution.py:45
  (132 shorter events, 79.7 us)
Async XLA Ops:
  7.2 109.9 %copy-start = (s32[4,4]{1,0:T(4,128)S(1)}, s32[4,4]{1,0:T(4,128)}, u32[]{:S(2)}) copy-start(s32[4,4]{1,0:T(4,128)} %param.14) | copy-start | bytes 196
  7.2 89.2 %all-gather.4.cloned.1.call-start = ((), (), s32[]{:S(2)}) async-start(), calls=%async_computation | async-start | bytes 5242880 | tf_op jit(solution)/shard_map/all_gather | solution.py:103
  8.6 52.0 %copy-start.17 = (s32[8,4]{0,1:T(4,128)S(1)}, s32[8,4]{0,1:T(4,128)}, u32[]{:S(2)}) copy-start(s32[8,4]{0,1:T(4,128)} %param.17) | copy-start | bytes 388
  8.6 52.9 %copy-start.11 = (f32[1024,768]{1,0:T(8,128)S(1)}, f32[1024,768]{1,0:T(8,128)}, u32[]{:S(2)}) copy-start(f32[1024,768]{1,0:T(8,128)} %param.12) | copy-start | bytes 9437188
  8.6 26.2 %collective-permute-start = (f32[256,1024]{1,0:T(8,128)S(1)}, f32[256,1024]{1,0:T(8,128)S(1)}, u32[]{:S(2)}, u32[]{:S(2)}) collective-permute-start(f32[256,1024]{1,0:T(8,128)S(1)} %constant_dynamic-slice_fusion.2), channel_id=1, source_target_pairs={{0,4},{4,0},{8,12},{12,8},{16,20},{20,16},{24,28},{28,24},{1,5},{5... | collective-permute-start | bytes 3145736 | tf_op jit(solution)/shard_map/ppermute | solution.py:10
  35.0 24.4 %collective-permute-start.1 = (f32[256,1024]{1,0:T(8,128)S(1)}, f32[256,1024]{1,0:T(8,128)S(1)}, u32[]{:S(2)}, u32[]{:S(2)}) collective-permute-start(f32[256,1024]{1,0:T(8,128)S(1)} %fusion.44), channel_id=1, source_target_pairs={{0,8},{4,12},{8,0},{12,4},{16,24},{20,28},{24,16},{28,20},{1,9},{5... | collective-permute-start | bytes 3145736 | tf_op jit(solution)/shard_map/ppermute | solution.py:10
  60.6 261.9 %all-reduce.3.cloned.1.call-start = ((), (), s32[]{:S(2)}) async-start(), calls=%async_computation.3 | async-start | bytes 24117248 | tf_op jit(solution)/shard_map/psum | solution.py:127
  110.2 237.4 %all-gather.8.cloned.1.call-start = ((), (), s32[]{:S(2)}) async-start(), calls=%async_computation.2 | async-start | bytes 2621440 | tf_op jit(solution)/shard_map/all_gather | solution.py:105
  144.0 73.7 %collective-permute-start.2 = (f32[256,2048]{0,1:T(8,128)}, f32[256,2048]{0,1:T(8,128)}, u32[]{:S(2)}, u32[]{:S(2)}) collective-permute-start(f32[256,2048]{0,1:T(8,128)} %fusion.6), channel_id=1, source_target_pairs={{0,4},{4,0},{8,12},{12,8},{16,20},{20,16},{24,28},{28,24},{1,5},{5... | collective-permute-start | bytes 6291464 | tf_op jit(solution)/shard_map/ppermute | solution.py:10
  148.1 55.0 %collective-permute-start.4 = (f32[512,256]{1,0:T(8,128)S(1)}, f32[512,256]{1,0:T(8,128)S(1)}, u32[]{:S(2)}, u32[]{:S(2)}) collective-permute-start(f32[512,256]{1,0:T(8,128)S(1)} %fusion.14), channel_id=1, source_target_pairs={{0,4},{4,0},{8,12},{12,8},{16,20},{20,16},{24,28},{28,24},{1,5},{5... | collective-permute-start | bytes 1572872 | tf_op jit(solution)/shard_map/ppermute | solution.py:10
  203.4 13.3 %collective-permute-start.5 = (f32[512,256]{1,0:T(8,128)S(1)}, f32[512,256]{1,0:T(8,128)S(1)}, u32[]{:S(2)}, u32[]{:S(2)}) collective-permute-start(f32[512,256]{1,0:T(8,128)S(1)} %fusion.43), channel_id=1, source_target_pairs={{0,8},{4,12},{8,0},{12,4},{16,24},{20,28},{24,16},{28,20},{1,9},{5... | collective-permute-start | bytes 1572872 | tf_op jit(solution)/shard_map/ppermute | solution.py:10
  217.6 340.9 %all-gather.6.cloned.1.call-start = ((), (), s32[]{:S(2)}) async-start(), calls=%async_computation.1 | async-start | bytes 10485760 | tf_op jit(solution)/shard_map/all_gather | solution.py:104
  220.3 46.2 %collective-permute-start.3 = (f32[256,2048]{0,1:T(8,128)S(1)}, f32[256,2048]{0,1:T(8,128)S(1)}, u32[]{:S(2)}, u32[]{:S(2)}) collective-permute-start(f32[256,2048]{0,1:T(8,128)S(1)} %fusion.42), channel_id=1, source_target_pairs={{0,8},{4,12},{8,0},{12,4},{16,24},{20,28},{24,16},{28,20},{1,9},{5... | collective-permute-start | bytes 6291464 | tf_op jit(solution)/shard_map/ppermute | solution.py:10
  322.5 300.8 %collective-permute-start.6 = (f32[1024,2048]{0,1:T(8,128)}, f32[1024,2048]{0,1:T(8,128)}, u32[]{:S(2)}, u32[]{:S(2)}) collective-permute-start(f32[1024,2048]{0,1:T(8,128)} %get-tuple-element.25), channel_id=1, source_target_pairs={{0,4},{4,0},{8,12},{12,8},{16,20},{20,16},{24,28},{28,24},{1,5},{5... | collective-permute-start | bytes 25165832 | tf_op jit(solution)/shard_map/ppermute | solution.py:10
  324.0 225.5 %collective-permute-start.7 = (f32[2048,256]{1,0:T(8,128)}, f32[2048,256]{1,0:T(8,128)}, u32[]{:S(2)}, u32[]{:S(2)}) collective-permute-start(f32[2048,256]{1,0:T(8,128)} %get-tuple-element.26), channel_id=1, source_target_pairs={{0,4},{4,0},{8,12},{12,8},{16,20},{20,16},{24,28},{28,24},{1,5},{5... | collective-permute-start | bytes 6291464 | tf_op jit(solution)/shard_map/ppermute | solution.py:10
  324.5 225.0 %copy-start.16 = (f32[2048,256]{1,0:T(8,128)S(1)}, f32[2048,256]{1,0:T(8,128)}, u32[]{:S(2)}) copy-start(f32[2048,256]{1,0:T(8,128)} %get-tuple-element.26) | copy-start | bytes 6291460
  558.5 25.9 %copy-start.5 = (f32[128,8,4,256]{3,1,2,0:T(8,128)S(1)}, f32[128,8,4,256]{3,1,2,0:T(8,128)}, u32[]{:S(2)}) copy-start(f32[128,8,4,256]{3,1,2,0:T(8,128)} %copy.55) | copy-start | bytes 12582916
  558.5 25.9 %copy-start.13 = (f32[1024,2048]{0,1:T(8,128)S(1)}, f32[1024,2048]{0,1:T(8,128)}, u32[]{:S(2)}) copy-start(f32[1024,2048]{0,1:T(8,128)} %all-gather.6.cloned.1.call-done) | copy-start | bytes 25165828
  622.2 18.5 %slice-start = ((s8[8388608]{0:T(1024)(128)(4,1)}), s8[4194304]{0:T(1024)(128)(4,1)S(1)}, s32[]{:S(2)}) async-start(s8[8388608]{0:T(1024)(128)(4,1)} %bitcast.80), calls=%async_computation.4 | async-start | bytes 8388608
  623.3 17.4 %slice-start.1 = ((s8[8388608]{0:T(1024)(128)(4,1)}), s8[4194304]{0:T(1024)(128)(4,1)S(1)}, s32[]{:S(2)}) async-start(s8[8388608]{0:T(1024)(128)(4,1)} %bitcast.80), calls=%async_computation.5 | async-start | bytes 8388608
  623.3 33.8 %slice-start.2 = ((s8[6291456]{0:T(1024)(128)(4,1)}), s8[4194304]{0:T(1024)(128)(4,1)S(1)}, s32[]{:S(2)}) async-start(s8[6291456]{0:T(1024)(128)(4,1)} %bitcast.82), calls=%async_computation.6 | async-start | bytes 8388608
  640.7 16.3 %slice-start.3 = ((s8[6291456]{0:T(1024)(128)(4,1)}), s8[2097152]{0:T(1024)(128)(4,1)S(1)}, s32[]{:S(2)}) async-start(s8[6291456]{0:T(1024)(128)(4,1)} %bitcast.82), calls=%async_computation.7 | async-start | bytes 4194304
  686.0 17.6 %copy-start.14 = (f32[1536,256]{1,0:T(8,128)S(1)}, f32[1536,256]{1,0:T(8,128)}, u32[]{:S(2)}) copy-start(f32[1536,256]{1,0:T(8,128)} %param.16) | copy-start | bytes 4718596
  686.0 18.9 %copy-start.1 = (s32[4,4]{1,0:T(4,128)S(1)}, s32[4,4]{1,0:T(4,128)}, u32[]{:S(2)}) copy-start(s32[4,4]{1,0:T(4,128)} %param.14) | copy-start | bytes 196
  (10 other events, 74.3 us)
Sparse Core Ops, SparseCore 0:
  60.7 35.6 all-gather.3
  110.3 212.1 all-reduce.2
  324.6 22.8 all-gather.7
  348.9 58.2 all-gather.5
where the time goes:
time: 720 us; the launch traced here: 712 us
  waiting for transfers between devices  430 us (60%)
  matrix products  143 us (20%)
  local copies, waits for them, and re-layouts  86.5 us (12%)
  other arithmetic  24.8 us (3%)
  between operations  14.7 us (2%)
  starting transfers between devices  12.9 us (2%)
    ppermute x8, waiting for transfers between devices, from_partner(): lax.ppermute(value, axis, [(i, i ^ 1 << bit) for i in range(lax.axis_size...  355 us
    psum x1, waiting for transfers between devices, local(): summed_terms = lax.psum(partial_value, 'rows')  54.4 us
    dot_general x2, matrix products, child_cov(): jnp.dot(parent_cov, chosen, precision=HIGH, preferred_element_type=jnp.fl...  43.3 us
    gather x4, local copies, waits for them, and re-layouts, select_blocks(): jnp.take(panel_cols.reshape(rows_total, local_count, block_size), wanted,...  30.7 us
    dot_general x2, matrix products, child_cov(): jnp.dot(chosen.T, product, precision=HIGH, preferred_element_type=jnp.flo...  30.3 us
    unnamed x55, local copies, waits for them, and re-layouts  28.7 us
    dot_general x3, matrix products, marg_terms(): jnp.einsum('sai,saj->aij', panel_cols.reshape(rows_total, block_count, bl...  27.1 us
    dot_general x1, matrix products, local(): jnp.dot(low_cov, panel_low, precision=HIGH, preferred_element_type=jnp.fl...  22.3 us
  transfers between devices with their start and end apart: 12, of which 9 were waited for; matrix products, arithmetic and copies ran while one was open for 22% of the time, Pallas kernels for 0%

commit v1 on v0

--- a/solution.py
+++ b/solution.py
@@ -124,7 +124,7 @@
     partial_value = marg_terms(panel_rows, cross_top, block_size)
     piece_rows = partial_value.shape[0] // row_count
     own_diag = lax.dynamic_slice_in_dim(diag_top, rows_index * piece_rows, piece_rows, 0)
-    summed_terms = lax.psum(partial_value, "rows")
+    summed_terms = jnp.sum(lax.all_gather(partial_value, "rows"), axis=0)
     marginal_top = own_diag - lax.dynamic_slice_in_dim(
         summed_terms, rows_index * piece_rows, piece_rows, 0
     )

time: 720 us -> 636 us (0.88)
  waiting for transfers between devices: 430 us -> 352 us
    psum x1, waiting for transfers between devices: 54.4 us -> 0.02 us  [local(): summed = lax.psum((chosen_mid, chosen_mid_diag), 'rows')]
    ppermute x8, waiting for transfers between devices: 355 us -> 333 us  [from_partner(): lax.ppermute(value, axis, [(i, i ^ 1 << bit) for i in range(lax.axis_size...]
    all_gather x1, waiting for transfers between devices: 16.3 us -> 2.39 us  [local(): lax.all_gather(pieces[2], 'rows', axis=0, tiled=True)]
    all_gather x1, waiting for transfers between devices: 3.92 us -> 16.1 us  [local(): lax.all_gather(pieces[0], 'rows', axis=0, tiled=True)]
    dot_general x2, matrix products: 43.3 us -> 35.1 us  [child_cov(): jnp.dot(parent_cov, chosen, precision=HIGH, preferred_element_type=jnp.fl...]
    unnamed x55 -> x45, local copies, waits for them, and re-layouts: 28.7 us -> 28.2 us
  transfers between devices with their start and end apart: 12 -> 13, of which waited for: 9 -> 8; matrix products, arithmetic and copies ran while one was open for 22% -> 34% of each run, Pallas kernels for 0% -> 0%
where the time goes in v1:
time: 636 us; the launch traced here: 629 us
  waiting for transfers between devices  352 us (55%)
  matrix products  138 us (22%)
  local copies, waits for them, and re-layouts  84.5 us (13%)
  other arithmetic  28 us (4%)
  between operations  14.4 us (2%)
  starting transfers between devices  12.1 us (2%)
    ppermute x8, waiting for transfers between devices, from_partner(): lax.ppermute(value, axis, [(i, i ^ 1 << bit) for i in range(lax.axis_size...  333 us
    dot_general x2, matrix products, child_cov(): jnp.dot(parent_cov, chosen, precision=HIGH, preferred_element_type=jnp.fl...  35.1 us
    dot_general x2, matrix products, child_cov(): jnp.dot(chosen.T, product, precision=HIGH, preferred_element_type=jnp.flo...  32.7 us
    gather x4, local copies, waits for them, and re-layouts, select_blocks(): jnp.take(panel_cols.reshape(rows_total, local_count, block_size), wanted,...  30 us
    unnamed x45, local copies, waits for them, and re-layouts  28.2 us
    dot_general x3, matrix products, marg_terms(): jnp.einsum('sai,saj->aij', panel_cols.reshape(rows_total, block_count, bl...  27 us
    dot_general x1, matrix products, local(): jnp.dot(low_cov, panel_low, precision=HIGH, preferred_element_type=jnp.fl...  22.1 us
    all_gather x1, waiting for transfers between devices, local(): lax.all_gather(pieces[0], 'rows', axis=0, tiled=True)  16.1 us
  transfers between devices with their start and end apart: 13, of which 8 were waited for; matrix products, arithmetic and copies ran while one was open for 34% of the time, Pallas kernels for 0%

profile of v1, /device:TPU:0, one launch (start us, length us, event | category | flops | bytes accessed | tf_op | source)
XLA Modules:
  0.0 629.1 jit_solution(7430282009033751968)
XLA Ops:
  19.1 9.2 %copy.61 = f32[1024,8,256]{0,2,1:T(8,128)} copy(f32[1024,8,256]{2,0,1:T(8,128)} %bitcast.66) | data formatting | bytes 16777216 | tf_op jit(solution)/shard_map/jit(_take)/gather | solution.py:25
  29.3 5.9 fusion
  41.5 23.2 %collective-permute-done = f32[256,1024]{1,0:T(8,128)S(1)} collective-permute-done((f32[256,1024]{1,0:T(8,128)S(1)}, f32[256,1024]{1,0:T(8,128)S(1)}, u32[]{:S(2)}, u32[]{:S(2)}) %collective-permute-start) | collective-permute-done | bytes 1048608 | tf_op jit(solution)/shard_map/ppermute | solution.py:10
  66.7 22.6 %collective-permute-done.1 = f32[256,1024]{1,0:T(8,128)S(1)} collective-permute-done((f32[256,1024]{1,0:T(8,128)S(1)}, f32[256,1024]{1,0:T(8,128)S(1)}, u32[]{:S(2)}, u32[]{:S(2)}) %collective-permute-start.1) | collective-permute-done | bytes 1048608 | tf_op jit(solution)/shard_map/ppermute | solution.py:10
  91.3 6.6 %copy.54 = f32[1024,1536]{0,1:T(8,128)} copy(f32[1024,1536]{1,0:T(8,128)} %param.10) | data formatting | bytes 12582912 | tf_op args[1]
  97.9 6.6 %copy.55 = f32[1024,6,256]{2,0,1:T(8,128)} copy(f32[1024,6,256]{0,2,1:T(8,128)} %bitcast.72) | data formatting | bytes 12582912 | tf_op jit(solution)/shard_map/reshape | solution.py:25
  104.6 7.2 %gather_fusion.1 = f32[8,1024,256]{2,1,0:T(8,128)} fusion(f32[1024,6,256]{2,0,1:T(8,128)} %copy.55, s32[1024]{0:T(1024)S(1)} %pad_clamp_fusion.2), kind=kCustom, calls=%fused_computation.1 | custom fusion | bytes 16777248 | tf_op jit(solution)/shard_map/jit(_take)/gather | solution.py:25
  111.8 9.2 %copy.56 = f32[1024,8,256]{0,2,1:T(8,128)} copy(f32[1024,8,256]{2,0,1:T(8,128)} %bitcast.67) | data formatting | bytes 16777216 | tf_op jit(solution)/shard_map/jit(_take)/gather | solution.py:25
  128.8 53.2 %collective-permute-done.4 = f32[512,256]{1,0:T(8,128)S(1)} collective-permute-done((f32[512,256]{1,0:T(8,128)S(1)}, f32[512,256]{1,0:T(8,128)S(1)}, u32[]{:S(2)}, u32[]{:S(2)}) %collective-permute-start.4) | collective-permute-done | bytes 524320 | tf_op jit(solution)/shard_map/ppermute | solution.py:10
  183.5 10.7 %collective-permute-done.5 = f32[512,256]{1,0:T(8,128)S(1)} collective-permute-done((f32[512,256]{1,0:T(8,128)S(1)}, f32[512,256]{1,0:T(8,128)S(1)}, u32[]{:S(2)}, u32[]{:S(2)}) %collective-permute-start.5) | collective-permute-done | bytes 524320 | tf_op jit(solution)/shard_map/ppermute | solution.py:10
  198.8 43.9 %collective-permute-done.3 = f32[256,2048]{0,1:T(8,128)S(1)} collective-permute-done((f32[256,2048]{0,1:T(8,128)S(1)}, f32[256,2048]{0,1:T(8,128)S(1)}, u32[]{:S(2)}, u32[]{:S(2)}) %collective-permute-start.3) | collective-permute-done | bytes 2097184 | tf_op jit(solution)/shard_map/ppermute | solution.py:10
  247.4 16.1 %all-gather.5.cloned.1.call-done = f32[1024,1024]{1,0:T(8,128)} async-done(((f32[256,1024]{1,0:T(8,128)}), f32[1024,1024]{1,0:T(8,128)}) %all-gather.5.cloned.1.call-update) | async-done | bytes 4194320 | tf_op jit(solution)/shard_map/all_gather | solution.py:103
  263.5 7.9 %convolution_negate_fusion.1 = f32[256,1536]{1,0:T(8,128)S(1)} fusion(f32[1024,1536]{1,0:T(8,128)} %param.10, f32[1024,1024]{1,0:T(8,128)} %all-gather.5.cloned.1.call-done, s32[]{:T(128)S(6)} %select_n.181), kind=kOutput, calls=%fused_computation.15 | convolution fusion | flops 4832231424 | bytes 8912900 | tf_op jit(solution)/shard_map/dot_general | solution.py:122
  279.1 6.7 %copy.63 = f32[1024,1536]{0,1:T(8,128)} copy(f32[1024,1536]{1,0:T(8,128)} %param.15) | data formatting | bytes 12582912 | tf_op args[6]
  289.5 179.4 %collective-permute-done.7 = f32[2048,256]{1,0:T(8,128)} collective-permute-done((f32[2048,256]{1,0:T(8,128)}, f32[2048,256]{1,0:T(8,128)}, u32[]{:S(2)}, u32[]{:S(2)}) %collective-permute-start.7) | collective-permute-done | bytes 2097184 | tf_op jit(solution)/shard_map/ppermute | solution.py:10
  478.0 17.3 %fusion.4 = f32[1024,1024]{1,0:T(8,128)S(1)} fusion(f32[1024,1024]{1,0:T(8,128)} %all-gather.5.cloned.1.call-done, f32[1024,2048]{0,1:T(8,128)} %all-gather.9.cloned.1.call-done, s32[]{:T(128)S(6)} %select_n.193), kind=kOutput, calls=%fused_computation.13 | convolution fusion | flops 12884901888 | bytes 12582916 | tf_op jit(solution)/shard_map/dot_general | solution.py:37
  495.3 16.1 %fusion.8 = f32[1024,1024]{1,0:T(8,128)S(1)} fusion(f32[1024,1024]{1,0:T(8,128)S(1)} %bitcast.75, f32[1024,1024]{1,0:T(8,128)S(1)} %fusion.4, f32[1024,2048]{0,1:T(8,128)} %all-gather.9.cloned.1.call-done, s32[]{:T(128)S(6)} %select_n.193), kind=kOutput, calls=%fused_computation.22 | convolution fusion | flops 12885950464 | bytes 16777220 | tf_op jit(solution)/shard_map/dot_general | solution.py:38
  511.5 17.8 %fusion.11 = f32[1024,1024]{1,0:T(8,128)S(1)} fusion(f32[1024,1024]{1,0:T(8,128)S(1)} %fusion.8, f32[1024,2048]{0,1:T(8,128)} %collective-permute-done.6, s32[]{:T(128)S(6)} %select_n.204, f32[1024,2048]{0,1:T(8,128)S(1)} %bitcast.81), kind=kOutput, calls=%fused_computation.25 | convolution fusion | flops 12885950464 | bytes 16777220 | tf_op jit(solution)/shard_map/dot_general | solution.py:37
  529.3 16.5 %fusion.12 = f32[1024,1024]{1,0:T(8,128)S(1)} fusion(f32[1024,1024]{1,0:T(8,128)S(1)} %fusion.11, f32[1024,2048]{0,1:T(8,128)} %collective-permute-done.6, s32[]{:T(128)S(6)} %select_n.204, f32[1024,2048]{0,1:T(8,128)S(1)} %bitcast.81), kind=kOutput, calls=%fused_computation.26 | convolution fusion | flops 12885950464 | bytes 16777220 | tf_op jit(solution)/shard_map/dot_general | solution.py:38
  545.9 22.1 %convolution_negate_fusion = f32[1024,1536]{1,0:T(8,128)} fusion(f32[1024,1536]{1,0:T(8,128)S(1)} %bitcast.83, f32[1024,1024]{1,0:T(8,128)S(1)} %fusion.12, f32[1024,1024]{1,0:T(8,128)S(1)} %bitcast.89), kind=kOutput, calls=%fused_computation.8 | convolution fusion | flops 19329974272 | bytes 20971520 | tf_op jit(solution)/shard_map/dot_general | solution.py:143
  568.0 6.7 %copy.62 = f32[1024,1536]{0,1:T(8,128)} copy(f32[1024,1536]{1,0:T(8,128)} %convolution_negate_fusion) | data formatting | bytes 12582912 | tf_op jit(solution)/shard_map/neg | solution.py:143
  574.7 13.6 %convolution_negate_fusion.2 = f32[1024,768]{0,1:T(8,128)} fusion(f32[1024,1024]{1,0:T(8,128)} %copy-done.3, f32[1024,768]{1,0:T(8,128)S(1)} %copy-done.9), kind=kOutput, calls=%fused_computation.23 | convolution fusion | flops 9664462848 | bytes 10485760 | tf_op jit(solution)/shard_map/dot_general | solution.py:137
  592.1 5.2 fusion.26
  598.3 17.4 %fusion.27 = f32[6,256,256]{1,2,0:T(8,128)S(1)} fusion(f32[1024,6,256]{0,2,1:T(8,128)} %bitcast.71, f32[1024,6,256]{0,2,1:T(8,128)} %bitcast.70), kind=kOutput, calls=%fused_computation.78 | convolution fusion | flops 4831838208 | bytes 14155776 | tf_op jit(solution)/shard_map/sai,saj->aij/dot_general | solution.py:45
  (126 shorter events, 73.2 us)
Async XLA Ops:
  7.2 83.4 %copy-start = (s32[4,4]{1,0:T(4,128)S(1)}, s32[4,4]{1,0:T(4,128)}, u32[]{:S(2)}) copy-start(s32[4,4]{1,0:T(4,128)} %param.14) | copy-start | bytes 196
  7.2 237.6 %all-reduce.3.cloned.1.call-start = ((), (), s32[]{:S(2)}) async-start(), calls=%async_computation.4 | async-start | bytes 20971520 | tf_op jit(solution)/shard_map/psum | solution.py:116
  19.1 9.6 %copy-start.5 = (f32[768,256]{1,0:T(8,128)S(1)}, f32[768,256]{1,0:T(8,128)}, u32[]{:S(2)}) copy-start(f32[768,256]{1,0:T(8,128)} %param.13) | copy-start | bytes 2359300
  37.0 226.4 %all-gather.5.cloned.1.call-start = ((), (), s32[]{:S(2)}) async-start(), calls=%async_computation | async-start | bytes 5242880 | tf_op jit(solution)/shard_map/all_gather | solution.py:103
  38.4 26.2 %collective-permute-start = (f32[256,1024]{1,0:T(8,128)S(1)}, f32[256,1024]{1,0:T(8,128)S(1)}, u32[]{:S(2)}, u32[]{:S(2)}) collective-permute-start(f32[256,1024]{1,0:T(8,128)S(1)} %constant_dynamic-slice_fusion.2), channel_id=1, source_target_pairs={{0,4},{4,0},{8,12},{12,8},{16,20},{20,16},{24,28},{28,24},{1,5},{5... | collective-permute-start | bytes 3145736 | tf_op jit(solution)/shard_map/ppermute | solution.py:10
  64.8 24.5 %collective-permute-start.1 = (f32[256,1024]{1,0:T(8,128)S(1)}, f32[256,1024]{1,0:T(8,128)S(1)}, u32[]{:S(2)}, u32[]{:S(2)}) collective-permute-start(f32[256,1024]{1,0:T(8,128)S(1)} %fusion.44), channel_id=1, source_target_pairs={{0,8},{4,12},{8,0},{12,4},{16,24},{20,28},{24,16},{28,20},{1,9},{5... | collective-permute-start | bytes 3145736 | tf_op jit(solution)/shard_map/ppermute | solution.py:10
  90.5 197.7 %all-gather.11.cloned.1.call-start = ((), (), s32[]{:S(2)}) async-start(), calls=%async_computation.3 | async-start | bytes 2621440 | tf_op jit(solution)/shard_map/all_gather | solution.py:105
  124.3 70.9 %collective-permute-start.2 = (f32[256,2048]{0,1:T(8,128)}, f32[256,2048]{0,1:T(8,128)}, u32[]{:S(2)}, u32[]{:S(2)}) collective-permute-start(f32[256,2048]{0,1:T(8,128)} %fusion.6), channel_id=1, source_target_pairs={{0,4},{4,0},{8,12},{12,8},{16,20},{20,16},{24,28},{28,24},{1,5},{5... | collective-permute-start | bytes 6291464 | tf_op jit(solution)/shard_map/ppermute | solution.py:10
  128.2 53.9 %collective-permute-start.4 = (f32[512,256]{1,0:T(8,128)S(1)}, f32[512,256]{1,0:T(8,128)S(1)}, u32[]{:S(2)}, u32[]{:S(2)}) collective-permute-start(f32[512,256]{1,0:T(8,128)S(1)} %fusion.14), channel_id=1, source_target_pairs={{0,4},{4,0},{8,12},{12,8},{16,20},{20,16},{24,28},{28,24},{1,5},{5... | collective-permute-start | bytes 1572872 | tf_op jit(solution)/shard_map/ppermute | solution.py:10
  182.3 12.0 %collective-permute-start.5 = (f32[512,256]{1,0:T(8,128)S(1)}, f32[512,256]{1,0:T(8,128)S(1)}, u32[]{:S(2)}, u32[]{:S(2)}) collective-permute-start(f32[512,256]{1,0:T(8,128)S(1)} %fusion.43), channel_id=1, source_target_pairs={{0,8},{4,12},{8,0},{12,4},{16,24},{20,28},{24,16},{28,20},{1,9},{5... | collective-permute-start | bytes 1572872 | tf_op jit(solution)/shard_map/ppermute | solution.py:10
  195.1 282.8 %all-gather.9.cloned.1.call-start = ((), (), s32[]{:S(2)}) async-start(), calls=%async_computation.2 | async-start | bytes 10485760 | tf_op jit(solution)/shard_map/all_gather | solution.py:104
  197.8 44.8 %collective-permute-start.3 = (f32[256,2048]{0,1:T(8,128)S(1)}, f32[256,2048]{0,1:T(8,128)S(1)}, u32[]{:S(2)}, u32[]{:S(2)}) collective-permute-start(f32[256,2048]{0,1:T(8,128)S(1)} %fusion.42), channel_id=1, source_target_pairs={{0,8},{4,12},{8,0},{12,4},{16,24},{20,28},{24,16},{28,20},{1,9},{5... | collective-permute-start | bytes 6291464 | tf_op jit(solution)/shard_map/ppermute | solution.py:10
  244.2 372.9 %all-gather.7.cloned.1.call-start = ((), (), s32[]{:S(2)}) async-start(), calls=%async_computation.1 | async-start | bytes 7864320 | tf_op jit(solution)/shard_map/all_gather | solution.py:127
  244.8 266.6 %collective-permute-start.6 = (f32[1024,2048]{0,1:T(8,128)}, f32[1024,2048]{0,1:T(8,128)}, u32[]{:S(2)}, u32[]{:S(2)}) collective-permute-start(f32[1024,2048]{0,1:T(8,128)} %get-tuple-element.30), channel_id=1, source_target_pairs={{0,4},{4,0},{8,12},{12,8},{16,20},{20,16},{24,28},{28,24},{1,5},{5... | collective-permute-start | bytes 25165832 | tf_op jit(solution)/shard_map/ppermute | solution.py:10
  277.5 191.4 %collective-permute-start.7 = (f32[2048,256]{1,0:T(8,128)}, f32[2048,256]{1,0:T(8,128)}, u32[]{:S(2)}, u32[]{:S(2)}) collective-permute-start(f32[2048,256]{1,0:T(8,128)} %get-tuple-element.31), channel_id=1, source_target_pairs={{0,4},{4,0},{8,12},{12,8},{16,20},{20,16},{24,28},{28,24},{1,5},{5... | collective-permute-start | bytes 6291464 | tf_op jit(solution)/shard_map/ppermute | solution.py:10
  279.1 189.8 %copy-start.12 = (f32[2048,256]{1,0:T(8,128)S(1)}, f32[2048,256]{1,0:T(8,128)}, u32[]{:S(2)}) copy-start(f32[2048,256]{1,0:T(8,128)} %get-tuple-element.31) | copy-start | bytes 6291460
  477.9 17.3 %copy-start.4 = (f32[128,8,4,256]{3,1,2,0:T(8,128)S(1)}, f32[128,8,4,256]{3,1,2,0:T(8,128)}, u32[]{:S(2)}) copy-start(f32[128,8,4,256]{3,1,2,0:T(8,128)} %copy.70) | copy-start | bytes 12582916
  477.9 33.5 %slice-start = ((s8[8388608]{0:T(1024)(128)(4,1)}), s8[4194304]{0:T(1024)(128)(4,1)S(1)}, s32[]{:S(2)}) async-start(s8[8388608]{0:T(1024)(128)(4,1)} %bitcast.80), calls=%async_computation.5 | async-start | bytes 8388608
  495.3 16.2 %slice-start.1 = ((s8[8388608]{0:T(1024)(128)(4,1)}), s8[4194304]{0:T(1024)(128)(4,1)S(1)}, s32[]{:S(2)}) async-start(s8[8388608]{0:T(1024)(128)(4,1)} %bitcast.80), calls=%async_computation.6 | async-start | bytes 8388608
  511.4 17.9 %copy-start.3 = (f32[1024,1024]{1,0:T(8,128)}, f32[1024,1024]{1,0:T(8,128)S(1)}, u32[]{:S(2)}) copy-start(f32[1024,1024]{1,0:T(8,128)S(1)} %fusion.8) | copy-start | bytes 12582916
  511.5 34.4 %slice-start.2 = ((s8[6291456]{0:T(1024)(128)(4,1)}), s8[4194304]{0:T(1024)(128)(4,1)S(1)}, s32[]{:S(2)}) async-start(s8[6291456]{0:T(1024)(128)(4,1)} %bitcast.82), calls=%async_computation.7 | async-start | bytes 8388608
  529.3 16.6 %slice-start.3 = ((s8[6291456]{0:T(1024)(128)(4,1)}), s8[2097152]{0:T(1024)(128)(4,1)S(1)}, s32[]{:S(2)}) async-start(s8[6291456]{0:T(1024)(128)(4,1)} %bitcast.82), calls=%async_computation.8 | async-start | bytes 4194304
  529.3 16.6 %copy-start.8 = (f32[128,8,4,256]{3,1,2,0:T(8,128)S(1)}, f32[128,8,4,256]{3,1,2,0:T(8,128)}, u32[]{:S(2)}) copy-start(f32[128,8,4,256]{3,1,2,0:T(8,128)} %copy.72) | copy-start | bytes 12582916
  598.3 17.4 %copy-start.10 = (f32[1536,256]{1,0:T(8,128)S(1)}, f32[1536,256]{1,0:T(8,128)}, u32[]{:S(2)}) copy-start(f32[1536,256]{1,0:T(8,128)} %param.16) | copy-start | bytes 4718596
  (6 other events, 29.6 us)
Sparse Core Ops, SparseCore 0:
  37.1 189.4 all-reduce.2
  228.8 34.6 all-gather.4
  265.6 22.5 all-gather.10
  289.6 58.2 all-gather.8
  349.3 46.3 all-gather.6
